TPU v7x, 32 devices: a whole 2x2x4 slice. The times are simulated.
32 devices in a mesh: bulk: 4 (over x, core), grid: 8 (over z, y).
Axes of the slice: x: 2, y: 2, z: 4, core: 2. Of those that a mesh axis runs over, the one named last changes fastest.
Arguments:
- offsets: float32 [8, 3, 4, 24, 128], P('grid', None, 'bulk'), may hold values from -0.75 to 0.75
- flow: float32 [8, 5, 4, 24, 128], P('grid', None, 'bulk'), may hold values from -6 to 6
- control_points: float32 [3, 16384], P(None, ('bulk', 'grid')), may hold values from -7 to 13
- rbf_weights: float32 [3, 16384], P(None, ('bulk', 'grid')), may hold values from -2 to 2
- peer_offset: int32 [8, 720, 1], P('grid', 'bulk'), may hold values from 0 to 6; in each aligned block of 180 rows (0 to 179, 180 to 359, ..., all dimensions but the last counted through in order) at most 28 rows name the same one
- donor_block: int32 [8, 720], P('grid', 'bulk'), may hold values from 0 to 23
- receptor_block: int32 [8, 720], P('grid', 'bulk'), may hold values from 0 to 23
Outputs:
- moved: float32 [8, 3, 4, 24, 128], P('grid', None, 'bulk')
- metric: float32 [8, 4, 24, 128], P('grid', 'bulk')
- fringe: float32 [8, 5, 4, 24, 128], P('grid', None, 'bulk')
Inputs may be any that keep to these rules, and one draw needn't show every extreme that they name: `peer_offset`: in the 180 rows of one device no value appears more than 28 times.
All inputs are finite; a program needn't handle non-finite values.
Results may differ from a plain program's by a relative error of at most 0.0003.
Values sent between devices are 32-bit elements; how exact they have to be, the bound alone decides.
A program may use at most 64 MiB of HBM per device.

v0:
```python
import math

import jax
import jax.numpy as jnp
from jax import lax
from jax.sharding import PartitionSpec as P

CAP = 28


HIGHEST = lax.Precision.HIGHEST
SUPPORT = 1.25
point_block = 2048


def padded_2(cells, sides, width):
    for axis, dim in sides:
        count = lax.axis_size(axis)
        head = lax.slice_in_dim(cells, 0, width, axis=dim)
        tail = lax.slice_in_dim(cells, cells.shape[dim] - width, cells.shape[dim], axis=dim)
        cells = jnp.concatenate(
            [
                lax.ppermute(tail, axis, [(i, (i + 1) % count) for i in range(count)]),
                cells,
                lax.ppermute(head, axis, [((i + 1) % count, i) for i in range(count)]),
            ],
            axis=dim,
        )
    return cells


def lattice(grid_ids, plane_ids, planes_total, radial, lines):
    theta = 2.0 * math.pi * plane_ids.astype(jnp.float32) / planes_total
    radius = 1.0 + 0.25 * jnp.arange(radial, dtype=jnp.float32)
    height = 0.1 * jnp.arange(lines, dtype=jnp.float32)
    centre = 0.5 * grid_ids.astype(jnp.float32)
    xcoord = (
        centre[:, None, None, None]
        + radius[None, None, :, None] * jnp.cos(theta)[None, :, None, None]
        + 0.0 * height[None, None, None, :]
    )
    ycoord = (radius[None, :, None] * jnp.sin(theta)[:, None, None] + 0.0 * height[None, None, :])[
        None
    ] + 0.0 * centre[:, None, None, None]
    zcoord = jnp.zeros_like(xcoord) + height[None, None, None, :]
    return jnp.stack([xcoord, ycoord, zcoord], axis=1)


def kernel_sum(nodes, points, weights):
    squared = (nodes[0][:, None] - points[0][None, :]) ** 2
    squared = squared + (nodes[1][:, None] - points[1][None, :]) ** 2
    squared = squared + (nodes[2][:, None] - points[2][None, :]) ** 2
    scaled = jnp.sqrt(squared) / SUPPORT
    inside = jnp.maximum(1.0 - scaled, 0.0)
    basis = inside**4 * (4.0 * scaled + 1.0)
    return jnp.einsum("ck,nk->cn", weights, basis, precision=HIGHEST)


def deck_terms(carry, nodes, points, weights):
    breadth = points.shape[1]
    tile_width = math.gcd(breadth, point_block)
    turns = breadth // tile_width

    def one_tile(tile_number, running):
        tile_points = lax.dynamic_slice_in_dim(points, tile_number * tile_width, tile_width, 1)
        tile_weights = lax.dynamic_slice_in_dim(weights, tile_number * tile_width, tile_width, 1)
        return running + kernel_sum(nodes, tile_points, tile_weights)

    return lax.fori_loop(0, turns, one_tile, carry)


def along_axis(field, axis):
    total = field.shape[axis]
    ahead = lax.slice_in_dim(field, 2, total, axis=axis)
    behind = lax.slice_in_dim(field, 0, total - 2, axis=axis)
    first = lax.slice_in_dim(field, 1, 2, axis=axis) - lax.slice_in_dim(field, 0, 1, axis=axis)
    last = lax.slice_in_dim(field, total - 1, total, axis=axis) - lax.slice_in_dim(
        field, total - 2, total - 1, axis=axis
    )
    return jnp.concatenate([first, (ahead - behind) * 0.5, last], axis=axis)


def jacobian(slope_plane, slope_radial, slope_height):
    cross_x = slope_radial[:, 1] * slope_height[:, 2] - slope_radial[:, 2] * slope_height[:, 1]
    cross_y = slope_radial[:, 2] * slope_height[:, 0] - slope_radial[:, 0] * slope_height[:, 2]
    cross_z = slope_radial[:, 0] * slope_height[:, 1] - slope_radial[:, 1] * slope_height[:, 0]
    return slope_plane[:, 0] * cross_x + slope_plane[:, 1] * cross_y + slope_plane[:, 2] * cross_z


def blend(receptor_xyz, donor_xyz, donor_values):
    squared = (receptor_xyz[:, 0, :, None] - donor_xyz[:, 0, None, :]) ** 2
    squared = squared + (receptor_xyz[:, 1, :, None] - donor_xyz[:, 1, None, :]) ** 2
    squared = squared + (receptor_xyz[:, 2, :, None] - donor_xyz[:, 2, None, :]) ** 2
    weight = 1.0 / (0.25 + squared)
    totals = jnp.sum(weight, axis=2)
    weighted = jnp.einsum("nad,nvd->nva", weight, donor_values, precision=HIGHEST)
    return weighted / totals[:, None, :]


def blend_group(items):
    receptor_xyz, donor = items
    return blend(receptor_xyz, donor[:, :3], donor[:, 3:])


def local(offsets, flow, control_points, rbf_weights, peer_offset, donor_block, receptor_block):
    planes = offsets.shape[2]
    radial = offsets.shape[3]
    lines = offsets.shape[4]
    blocks = planes * radial
    grids = lax.axis_size("grid")
    grid_here = lax.axis_index("grid")
    plane_ids = lax.axis_index("bulk") * planes + jnp.arange(planes, dtype=jnp.int32)
    base = (
        lattice(grid_here[None], plane_ids, planes * lax.axis_size("bulk"), radial, lines) + offsets
    )
    nodes = base[0].reshape(3, -1)
    empty = jnp.zeros(nodes.shape, jnp.float32)
    all_points, all_weights = (
        lax.all_gather(control_points, ("bulk", "grid"), axis=1, tiled=True),
        lax.all_gather(rbf_weights, ("bulk", "grid"), axis=1, tiled=True),
    )
    shifts = deck_terms(empty, nodes, all_points, all_weights)
    moved = base + shifts.reshape(base.shape)
    padded = padded_2(moved, (("bulk", 2),), 1)
    slope_plane = (padded[:, :, 2:] - padded[:, :, :-2]) * 0.5
    slope_radial = along_axis(moved, 3)
    slope_height = along_axis(moved, 4)
    metric = jacobian(slope_plane, slope_radial, slope_height)
    values = metric[:, None] * flow
    payload = jnp.concatenate([moved, values], axis=1)[0].reshape(-1, blocks, lines)
    coords = moved[0].reshape(3, blocks, lines)
    block_iota = jnp.arange(blocks, dtype=jnp.int32)
    pick_donor = (donor_block[0][:, None] == block_iota[None, :]).astype(jnp.float32)
    chosen = jnp.einsum("sb,cbk->sck", pick_donor, payload, precision=HIGHEST)
    receiver = (grid_here + 1 + peer_offset[0, :, 0]) % grids
    receiver_hot = (receiver[:, None] == jnp.arange(grids, dtype=jnp.int32)[None, :]).astype(
        jnp.int32
    )
    before = jnp.cumsum(receiver_hot, axis=0) - receiver_hot
    position = jnp.sum(before * receiver_hot, axis=1)
    capacity = CAP
    target = receiver * capacity + position
    place = (jnp.arange(grids * capacity, dtype=jnp.int32)[:, None] == target[None, :]).astype(
        jnp.float32
    )
    label = (receptor_block[0] + 1).astype(jnp.float32)
    label_sent = jnp.einsum("ts,s->t", place, label, precision=HIGHEST).reshape(grids, capacity)
    sent = jnp.einsum("ts,sck->tck", place, chosen, precision=HIGHEST).reshape(
        grids, capacity, -1, lines
    )
    arrived, arrived_label = (
        lax.all_to_all(sent, "grid", split_axis=0, concat_axis=0, tiled=True),
        lax.all_to_all(label_sent, "grid", split_axis=0, concat_axis=0, tiled=True),
    )
    pick_receptor = (
        arrived_label.reshape(-1)[:, None] == (block_iota + 1).astype(jnp.float32)[None, :]
    ).astype(jnp.float32)
    receptor_xyz = jnp.einsum("tb,cbk->tck", pick_receptor, coords, precision=HIGHEST).reshape(
        grids, capacity, 3, lines
    )
    interpolated = lax.map(blend_group, (receptor_xyz, arrived)).reshape(
        grids * capacity, -1, lines
    )
    fringe = jnp.einsum("tb,tvk->vbk", pick_receptor, interpolated, precision=HIGHEST)
    return (moved, metric, fringe.reshape(1, -1, planes, radial, lines))


def solution(mesh):
    in_specs = (
        P("grid", None, "bulk", None, None),
        P("grid", None, "bulk", None, None),
        P(None, ("bulk", "grid")),
        P(None, ("bulk", "grid")),
        P("grid", "bulk", None),
        P("grid", "bulk"),
        P("grid", "bulk"),
    )
    out_specs = (
        P("grid", None, "bulk", None, None),
        P("grid", "bulk", None, None),
        P("grid", None, "bulk", None, None),
    )
    return jax.shard_map(local, mesh=mesh, in_specs=in_specs, out_specs=out_specs, check_vma=False)
```

profile of v0, /device:TPU:0, one launch (start us, length us, event | category | flops | bytes accessed | tf_op | source)
XLA Modules:
  0.0 534.4 jit_solution(6957581617032053949)
XLA Ops:
  1.7 71.5 %all_gather.7 = f32[3,16384]{1,0:T(4,128)S(1)} all-gather(f32[3,512]{1,0:T(4,128)} %param.13), channel_id=1, replica_groups=mesh['bulk'=4,'grid'=8] {'bulk','grid'}, dimensions={1}, use_global_device_ids=true | all-gather | bytes 202752 | tf_op jit(solution)/shard_map/all_gather | solution.py:119
  73.2 65.0 %all_gather.6 = f32[3,16384]{1,0:T(4,128)S(1)} all-gather(f32[3,512]{1,0:T(4,128)} %param.14), channel_id=1, replica_groups=mesh['bulk'=4,'grid'=8] {'bulk','grid'}, dimensions={1}, use_global_device_ids=true | all-gather | bytes 202752 | tf_op jit(solution)/shard_map/all_gather | solution.py:120
  138.2 300.2 %while.27 = (s32[]{:T(128)}, f32[3,3072]{1,0:T(4,128)S(1)}, f32[3,16384]{1,0:T(4,128)S(1)}, f32[3,3072]{1,0:T(4,128)S(1)}, f32[3,16384]{1,0:T(4,128)S(1)}, /*ind...) while((s32[]{:T(128)}, f32[3,3072]{1,0:T(4,128)S(1)}, ...), condition=%wide.region_1.0_spmd.clone, body=%wide.region_0.0_spmd.clone.sunk | while | flops 327174144 | bytes 303317 | solution.py:69
  138.3 37.3 %fusion.98 = f32[3,3072]{1,0:T(4,128)S(1)} fusion(f32[2048]{0:T(1024)S(1)} %bitcast.128, f32[3072]{0:T(1024)S(1)} %bitcast.124, f32[2048]{0:T(1024)S(1)} %bitcast.127, f32[3072]{0:T(1024)S(1)} %bitcast.125, f32[2048]{0:T(1024)S(1)} %bitcast.126, f32[3072]{0:T(1024)S(1)} %bitcast.123, f32[3,3072]{1,0:T(4,128)S(1)} %get-tuple-element.325, ...), kind=kOutput, calls=%fused_computation.44.clone.1 | convolution fusion | flops 327174144 | bytes 180229 | tf_op jit(solution)/shard_map/while/body/eval_jaxpr/ck,nk->cn/dot_general | solution.py:56
  175.8 37.3 %fusion.98 = f32[3,3072]{1,0:T(4,128)S(1)} fusion(f32[2048]{0:T(1024)S(1)} %bitcast.128, f32[3072]{0:T(1024)S(1)} %bitcast.124, f32[2048]{0:T(1024)S(1)} %bitcast.127, f32[3072]{0:T(1024)S(1)} %bitcast.125, f32[2048]{0:T(1024)S(1)} %bitcast.126, f32[3072]{0:T(1024)S(1)} %bitcast.123, f32[3,3072]{1,0:T(4,128)S(1)} %get-tuple-element.325, ...), kind=kOutput, calls=%fused_computation.44.clone.1 | convolution fusion | flops 327174144 | bytes 180229 | tf_op jit(solution)/shard_map/while/body/eval_jaxpr/ck,nk->cn/dot_general | solution.py:56
  213.3 37.3 %fusion.98 = f32[3,3072]{1,0:T(4,128)S(1)} fusion(f32[2048]{0:T(1024)S(1)} %bitcast.128, f32[3072]{0:T(1024)S(1)} %bitcast.124, f32[2048]{0:T(1024)S(1)} %bitcast.127, f32[3072]{0:T(1024)S(1)} %bitcast.125, f32[2048]{0:T(1024)S(1)} %bitcast.126, f32[3072]{0:T(1024)S(1)} %bitcast.123, f32[3,3072]{1,0:T(4,128)S(1)} %get-tuple-element.325, ...), kind=kOutput, calls=%fused_computation.44.clone.1 | convolution fusion | flops 327174144 | bytes 180229 | tf_op jit(solution)/shard_map/while/body/eval_jaxpr/ck,nk->cn/dot_general | solution.py:56
  250.8 37.3 %fusion.98 = f32[3,3072]{1,0:T(4,128)S(1)} fusion(f32[2048]{0:T(1024)S(1)} %bitcast.128, f32[3072]{0:T(1024)S(1)} %bitcast.124, f32[2048]{0:T(1024)S(1)} %bitcast.127, f32[3072]{0:T(1024)S(1)} %bitcast.125, f32[2048]{0:T(1024)S(1)} %bitcast.126, f32[3072]{0:T(1024)S(1)} %bitcast.123, f32[3,3072]{1,0:T(4,128)S(1)} %get-tuple-element.325, ...), kind=kOutput, calls=%fused_computation.44.clone.1 | convolution fusion | flops 327174144 | bytes 180229 | tf_op jit(solution)/shard_map/while/body/eval_jaxpr/ck,nk->cn/dot_general | solution.py:56
  288.3 37.3 %fusion.98 = f32[3,3072]{1,0:T(4,128)S(1)} fusion(f32[2048]{0:T(1024)S(1)} %bitcast.128, f32[3072]{0:T(1024)S(1)} %bitcast.124, f32[2048]{0:T(1024)S(1)} %bitcast.127, f32[3072]{0:T(1024)S(1)} %bitcast.125, f32[2048]{0:T(1024)S(1)} %bitcast.126, f32[3072]{0:T(1024)S(1)} %bitcast.123, f32[3,3072]{1,0:T(4,128)S(1)} %get-tuple-element.325, ...), kind=kOutput, calls=%fused_computation.44.clone.1 | convolution fusion | flops 327174144 | bytes 180229 | tf_op jit(solution)/shard_map/while/body/eval_jaxpr/ck,nk->cn/dot_general | solution.py:56
  325.8 37.3 %fusion.98 = f32[3,3072]{1,0:T(4,128)S(1)} fusion(f32[2048]{0:T(1024)S(1)} %bitcast.128, f32[3072]{0:T(1024)S(1)} %bitcast.124, f32[2048]{0:T(1024)S(1)} %bitcast.127, f32[3072]{0:T(1024)S(1)} %bitcast.125, f32[2048]{0:T(1024)S(1)} %bitcast.126, f32[3072]{0:T(1024)S(1)} %bitcast.123, f32[3,3072]{1,0:T(4,128)S(1)} %get-tuple-element.325, ...), kind=kOutput, calls=%fused_computation.44.clone.1 | convolution fusion | flops 327174144 | bytes 180229 | tf_op jit(solution)/shard_map/while/body/eval_jaxpr/ck,nk->cn/dot_general | solution.py:56
  363.3 37.3 %fusion.98 = f32[3,3072]{1,0:T(4,128)S(1)} fusion(f32[2048]{0:T(1024)S(1)} %bitcast.128, f32[3072]{0:T(1024)S(1)} %bitcast.124, f32[2048]{0:T(1024)S(1)} %bitcast.127, f32[3072]{0:T(1024)S(1)} %bitcast.125, f32[2048]{0:T(1024)S(1)} %bitcast.126, f32[3072]{0:T(1024)S(1)} %bitcast.123, f32[3,3072]{1,0:T(4,128)S(1)} %get-tuple-element.325, ...), kind=kOutput, calls=%fused_computation.44.clone.1 | convolution fusion | flops 327174144 | bytes 180229 | tf_op jit(solution)/shard_map/while/body/eval_jaxpr/ck,nk->cn/dot_general | solution.py:56
  400.8 37.3 %fusion.98 = f32[3,3072]{1,0:T(4,128)S(1)} fusion(f32[2048]{0:T(1024)S(1)} %bitcast.128, f32[3072]{0:T(1024)S(1)} %bitcast.124, f32[2048]{0:T(1024)S(1)} %bitcast.127, f32[3072]{0:T(1024)S(1)} %bitcast.125, f32[2048]{0:T(1024)S(1)} %bitcast.126, f32[3072]{0:T(1024)S(1)} %bitcast.123, f32[3,3072]{1,0:T(4,128)S(1)} %get-tuple-element.325, ...), kind=kOutput, calls=%fused_computation.44.clone.1 | convolution fusion | flops 327174144 | bytes 180229 | tf_op jit(solution)/shard_map/while/body/eval_jaxpr/ck,nk->cn/dot_general | solution.py:56
  442.3 3.5 all-to-all-start.1
  448.9 3.3 all-to-all-done.1
  452.2 3.6 all-to-all-start
  457.5 19.4 %all-to-all-done = f32[8,28,8,128]{3,2,1,0:T(8,128)S(1)} async-done(((f32[8,28,8,128]{3,2,1,0:T(8,128)}), f32[8,28,8,128]{3,2,1,0:T(8,128)S(1)}, u32[]{:S(2)}, u32[]{:S(2)}) %all-to-all-start) | async-done | bytes 917536 | tf_op jit(solution)/shard_map/all_to_all | solution.py:152
  476.9 56.5 %while.26 = (s32[]{:T(128)}, f32[8,28,5,128]{3,2,1,0:T(8,128)S(1)}, f32[8,28,8,128]{3,2,1,0:T(8,128)S(1)}, f32[8,28,3,128]{3,1,2,0:T(8,128)S(1)}, s32[]{:T(128)}) while((s32[]{:T(128)}, f32[8,28,5,128]{3,2,1,0:T(8,128)S(1)}, f32[8,28,8,128]{3,2,1,0:T(8,128)S(1)}, f32[8,28,3,128]{3,1,2,0:T(8,128)S(1)}, s32[]{:T(128)}) %tuple.87), condition=%wide.region_7.8_spmd, body=%wide.region_5.7_spmd.sunk | while | flops 37173248 | bytes 1017937 | solution.py:161
  476.9 2.4 fusion.93
  479.4 4.5 fusion.94
  484.0 2.4 fusion.93
  486.5 4.5 fusion.94
  491.1 2.4 fusion.93
  493.5 4.5 fusion.94
  498.2 2.4 fusion.93
  500.6 4.5 fusion.94
  505.2 2.4 fusion.93
  507.7 4.5 fusion.94
  512.3 2.4 fusion.93
  514.7 4.5 fusion.94
  519.4 2.4 fusion.93
  521.8 4.5 fusion.94
  526.4 2.4 fusion.93
  528.9 4.5 fusion.94
  (115 shorter events, 12.1 us)
Async XLA Ops:
  138.2 300.2 %copy-start.1 = (f32[1,3,1,24,128]{4,3,2,1,0:T(8,128)S(1)}, f32[1,3,1,24,128]{4,3,2,1,0:T(8,128)}, u32[]{:S(2)}) copy-start(f32[1,3,1,24,128]{4,3,2,1,0:T(8,128)} %param.11) | copy-start | bytes 110596
  138.2 302.1 %copy-start.5 = (s32[1,180,1]{1,2,0:T(1,128)S(1)}, s32[1,180,1]{1,2,0:T(1,128)}, u32[]{:S(2)}) copy-start(s32[1,180,1]{1,2,0:T(1,128)} %param.15) | copy-start | bytes 2164
  138.2 303.1 %copy-start.6 = (s32[1,180]{1,0:T(1,128)S(1)}, s32[1,180]{1,0:T(1,128)}, u32[]{:S(2)}) copy-start(s32[1,180]{1,0:T(1,128)} %param.17) | copy-start | bytes 2164
  438.4 7.8 %copy-start.2 = (f32[1,5,1,24,128]{4,3,2,1,0:T(8,128)S(1)}, f32[1,5,1,24,128]{4,3,2,1,0:T(8,128)}, u32[]{:S(2)}) copy-start(f32[1,5,1,24,128]{4,3,2,1,0:T(8,128)} %param.12) | copy-start | bytes 184324
  438.4 7.8 %copy-start.4 = (s32[1,180]{1,0:T(1,128)S(1)}, s32[1,180]{1,0:T(1,128)}, u32[]{:S(2)}) copy-start(s32[1,180]{1,0:T(1,128)} %param.16) | copy-start | bytes 2164
  438.4 18.6 %copy-start = (f32[1,3,1,24,128]{4,3,1,2,0:T(8,128)}, f32[1,3,1,24,128]{4,3,1,2,0:T(8,128)S(1)}, u32[]{:S(2)}) copy-start(f32[1,3,1,24,128]{4,3,1,2,0:T(8,128)S(1)} %bitcast_add_fusion) | copy-start | bytes 110596
  438.4 7.7 %collective-permute-start.1 = (f32[1,3,1,24,128]{4,3,1,2,0:T(8,128)S(1)}, f32[1,3,1,24,128]{4,3,1,2,0:T(8,128)S(1)}, u32[]{:S(2)}, u32[]{:S(2)}) collective-permute-start(f32[1,3,1,24,128]{4,3,1,2,0:T(8,128)S(1)} %bitcast_add_fusion), channel_id=1, source_target_pairs={{0,8},{8,16},{16,24},{24,0},{1,9},{9,17},{17,25},{25,1},{2,10},{10... | collective-permute-start | bytes 110600 | tf_op jit(solution)/shard_map/ppermute | solution.py:23
  438.5 7.6 %collective-permute-start = (f32[1,3,1,24,128]{4,3,1,2,0:T(8,128)S(1)}, f32[1,3,1,24,128]{4,3,1,2,0:T(8,128)S(1)}, u32[]{:S(2)}, u32[]{:S(2)}) collective-permute-start(f32[1,3,1,24,128]{4,3,1,2,0:T(8,128)S(1)} %bitcast_add_fusion), channel_id=1, source_target_pairs={{8,0},{16,8},{24,16},{0,24},{9,1},{17,9},{25,17},{1,25},{10,2},{18... | collective-permute-start | bytes 110600 | tf_op jit(solution)/shard_map/ppermute | solution.py:25
  442.3 9.9 %all-to-all-start.1 = ((f32[8,1,28]{2,1,0:T(1,128)}), f32[8,1,28]{2,1,0:T(1,128)S(1)}, u32[]{:S(2)}, u32[]{:S(2)}) async-start(f32[8,1,28]{2,1,0:T(1,128)} %convolution_bitcast_fusion.1), calls=%async_computation.1 | async-start | bytes 8192 | tf_op jit(solution)/shard_map/all_to_all | solution.py:153
  446.2 1.2 copy-start.3
  452.2 24.7 %all-to-all-start = ((f32[8,28,8,128]{3,2,1,0:T(8,128)}), f32[8,28,8,128]{3,2,1,0:T(8,128)S(1)}, u32[]{:S(2)}, u32[]{:S(2)}) async-start(f32[8,28,8,128]{3,2,1,0:T(8,128)} %bitcast.19), calls=%async_computation | async-start | bytes 1835008 | tf_op jit(solution)/shard_map/all_to_all | solution.py:152
where the time goes:
time: 535 us; the launch traced here: 534 us
  matrix products  339 us (63%)
  blocking collectives  136 us (25%)
  waiting for transfers between devices  22.7 us (4%)
  other arithmetic  22.2 us (4%)
  starting transfers between devices  8.83 us (2%)
    dot_general x8, matrix products, kernel_sum(): return jnp.einsum('ck,nk->cn', weights, basis, precision=HIGHEST)  299 us
    all_gather x1, blocking collectives, local(): lax.all_gather(control_points, ('bulk', 'grid'), axis=1, tiled=True)  71.5 us
    all_gather x1, blocking collectives, local(): lax.all_gather(rbf_weights, ('bulk', 'grid'), axis=1, tiled=True)  65 us
    dot_general x8, matrix products, blend(): jnp.einsum('nad,nvd->nva', weight, donor_values, precision=HIGHEST)  36.2 us
    reduce_sum x8, other arithmetic, blend(): totals = jnp.sum(weight, axis=2)  19.5 us
    all_to_all x1, waiting for transfers between devices, local(): lax.all_to_all(sent, 'grid', split_axis=0, concat_axis=0, tiled=True)  19.4 us
  transfers between devices with their start and end apart: 4, of which 2 were waited for; matrix products, arithmetic and copies ran while one was open for 1% of the time, Pallas kernels for 0%

commit v1 on v0

v1 whole, which is shorter than its diff:
```python
import functools
import math

import jax
import jax.numpy as jnp
from jax import lax
from jax.experimental import pallas as pl
from jax.experimental.pallas import tpu as pltpu
from jax.sharding import PartitionSpec as P

MESH = pl.DeviceIdType.MESH
SUPPORT = 1.25
CULL = SUPPORT * SUPPORT * 1.0001
FAR = 1.0e9
UNROLL = 16
ENTRY_UNROLL = 2
F32 = jnp.float32
I32 = jnp.int32
BF16 = jnp.bfloat16
VMEM_SPEC = pl.BlockSpec(memory_space=pltpu.VMEM)
SMEM_SPEC = pl.BlockSpec(memory_space=pltpu.SMEM)


def lattice(grid_ids, plane_ids, planes_total, radial, lines):
    theta = 2.0 * math.pi * plane_ids.astype(jnp.float32) / planes_total
    radius = 1.0 + 0.25 * jnp.arange(radial, dtype=jnp.float32)
    height = 0.1 * jnp.arange(lines, dtype=jnp.float32)
    centre = 0.5 * grid_ids.astype(jnp.float32)
    xcoord = (
        centre[:, None, None, None]
        + radius[None, None, :, None] * jnp.cos(theta)[None, :, None, None]
        + 0.0 * height[None, None, None, :]
    )
    ycoord = (radius[None, :, None] * jnp.sin(theta)[:, None, None] + 0.0 * height[None, None, :])[
        None
    ] + 0.0 * centre[:, None, None, None]
    zcoord = jnp.zeros_like(xcoord) + height[None, None, None, :]
    return jnp.stack([xcoord, ycoord, zcoord], axis=1)


def take_lanes(x, idx):
    dims = lax.GatherDimensionNumbers(
        offset_dims=(),
        collapsed_slice_dims=(1,),
        start_index_map=(1,),
        operand_batching_dims=(0,),
        start_indices_batching_dims=(0,),
    )
    return lax.gather(
        x, idx[..., None], dims, slice_sizes=(1, 1), mode=lax.GatherScatterMode.PROMISE_IN_BOUNDS
    )


def iota(shape, axis):
    return lax.broadcasted_iota(I32, shape, axis)


def search(counts, target):
    pos = jnp.zeros(counts.shape, I32)
    step = counts.shape[1] // 2
    while step:
        seen = take_lanes(counts, pos + (step - 1))
        pos = jnp.where(seen <= target, pos + step, pos)
        step //= 2
    return pos


def gather_kernel(nb, ng, pts_ref, lst_ref, allp_ref, alll_ref, sp, rp, sl, rl):
    b = lax.axis_index("bulk")
    g = lax.axis_index("grid")
    nd = nb * ng
    me = b * ng + g
    barrier = pltpu.get_barrier_semaphore()

    def peer_of(k):
        peer = lax.rem(me + k, nd)
        return (peer // ng, lax.rem(peer, ng))

    @pl.loop(1, nd)
    def _(k):
        pl.semaphore_signal(barrier, inc=1, device_id=peer_of(k), device_id_type=MESH)

    pl.semaphore_wait(barrier, nd - 1)

    def points_copy(k, slot):
        return pltpu.make_async_remote_copy(
            src_ref=pts_ref,
            dst_ref=allp_ref.at[slot],
            send_sem=sp.at[k - 1],
            recv_sem=rp.at[k - 1],
            device_id=peer_of(k),
            device_id_type=MESH,
        )

    def list_copy(k):
        return pltpu.make_async_remote_copy(
            src_ref=lst_ref,
            dst_ref=alll_ref.at[k - 1],
            send_sem=sl.at[k - 1],
            recv_sem=rl.at[k - 1],
            device_id=(b, lax.rem(g + k, ng)),
            device_id_type=MESH,
        )

    @pl.loop(1, nd)
    def _(k):
        points_copy(k, me).start()

    @pl.loop(1, ng)
    def _(k):
        list_copy(k).start()

    allp_ref[me] = pts_ref[...]

    @pl.loop(1, nd)
    def _(k):
        copy = points_copy(k, lax.rem(me + nd - k, nd))
        copy.wait_send()
        copy.wait_recv()

    @pl.loop(1, ng)
    def _(k):
        copy = list_copy(k)
        copy.wait_send()
        copy.wait_recv()


def rbf_kernel(
    nd,
    rows,
    ng,
    lrows,
    base_ref,
    pts_ref,
    lst_ref,
    moved_ref,
    don_ref,
    rec_ref,
    num_ref,
    pnt,
    fil,
    node,
    box,
    out,
    basec,
    cntv,
    cnts,
    shift,
    names,
    sem,
):
    radial = base_ref.shape[1]
    npat = radial
    lane8 = iota((8, 128), 1)
    sub8 = iota((8, 128), 0)
    blocks_of_lanes = lane8 // 16
    within = lane8 - 16 * blocks_of_lanes
    upper = (iota((128, 128), 0) <= iota((128, 128), 1)).astype(F32).astype(BF16)

    def running(mask):
        return jnp.dot(
            mask.astype(F32).astype(BF16), upper, preferred_element_type=F32
        ).astype(I32)

    nrow = (ng - 1) * lrows
    for k in range(ng - 1):
        for c in range(3):
            names[c, k * lrows : (k + 1) * lrows, :] = lst_ref[k, c * lrows : (c + 1) * lrows, :]
    owner = iota((nrow, 128), 0) // lrows
    counts = running(names[0] == owner)
    pos = search(counts, iota((nrow, 128), 1))
    don_ref[...] = owner * radial + take_lanes(names[1], pos)
    rec_ref[...] = take_lanes(names[2], pos)
    num_ref[...] = take_lanes(counts, jnp.full((nrow, 128), 127, I32))

    for d in range(nd):
        for c in range(6):
            pnt[c, d * rows : (d + 1) * rows, :] = pts_ref[d, c * rows : (c + 1) * rows, :]

    lows, highs = [], []
    for c in range(3):
        for jg in range(radial // 8):
            v = base_ref[c, 8 * jg : 8 * jg + 8, :]
            got = jnp.zeros((8, 128), F32)
            for j in range(8):
                row = jnp.broadcast_to(v[j : j + 1, :], (8, 128))
                got = jnp.where(blocks_of_lanes == j, take_lanes(row, 16 * sub8 + within), got)
            node[c, 8 * jg : 8 * jg + 8, :] = got
        full = node[c]
        lo = jnp.min(full, axis=1, keepdims=True)
        hi = jnp.max(full, axis=1, keepdims=True)
        box[2 * c] = jnp.broadcast_to(lo[:, :, None], (npat, 8, 128))
        box[2 * c + 1] = jnp.broadcast_to(hi[:, :, None], (npat, 8, 128))
        lows.append(jnp.min(lo, axis=0, keepdims=True))
        highs.append(jnp.max(hi, axis=0, keepdims=True))

    dist = jnp.zeros((128, 128), F32)
    for c in range(3):
        p = pnt[c]
        e = jnp.maximum(jnp.maximum(lows[c] - p, p - highs[c]), 0.0)
        dist = dist + e * e
    counts = running(dist < CULL)
    lane = iota((128, 128), 1)
    pos = search(counts, lane)
    total = take_lanes(counts, jnp.full((128, 128), 127, I32))
    for c in range(6):
        v = take_lanes(pnt[c], pos)
        v = jnp.where(lane < total, v, FAR if c < 3 else 0.0)
        fil[c] = v.T
    groups = (jnp.max(total) + 7) // 8

    shift[...] = jnp.zeros(shift.shape, F32)
    wide = npat * 8
    lane_w = iota((wide, 128), 1)

    def page_body(state):
        page, _ = state
        basec[...] = jnp.zeros(basec.shape, I32)
        out[...] = jnp.zeros(out.shape, F32)

        @pl.loop(0, groups)
        def _(gi):
            start = pl.multiple_of(gi * 8, 8)
            dist = jnp.zeros((npat, 8, 128), F32)
            for c in range(3):
                p = fil[c, pl.ds(start, 8), :][None]
                e = jnp.maximum(jnp.maximum(box[2 * c] - p, p - box[2 * c + 1]), 0.0)
                dist = dist + e * e
            before = basec[...]
            counts = before + running((dist < CULL).astype(F32).reshape(wide, 128))
            target = lane_w + 128 * page
            pos = search(counts, target)
            after = take_lanes(counts, jnp.full((wide, 128), 127, I32))
            keep = jnp.logical_and(target >= before, target < after)
            for c in range(6):
                src = jnp.broadcast_to(
                    fil[c, pl.ds(start, 8), :][None], (npat, 8, 128)
                ).reshape(wide, 128)
                out[c] = jnp.where(keep, take_lanes(src, pos), out[c])
            basec[...] = after

        most = jnp.max(basec[...].reshape(npat, 8, 128), axis=1)
        cntv[...] = most
        copy = pltpu.make_async_copy(cntv, cnts, sem)
        copy.start()
        copy.wait()

        @pl.loop(0, npat)
        def _(p):
            n = jnp.minimum(cnts[p, 0] - 128 * page, 128)
            turns = (jnp.maximum(n, 0) + (UNROLL - 1)) // UNROLL
            at = [jnp.broadcast_to(node[c, pl.ds(p, 1), :] * 0.8, (8, 128)) for c in range(3)]
            first = pl.multiple_of(p * 8, 8)
            cols = [out[c, pl.ds(first, 8), :] for c in range(6)]
            cols = [v * 0.8 for v in cols[:3]] + cols[3:]

            def step(i, acc):
                acc = list(acc)
                for u in range(UNROLL):
                    idx = jnp.full((8, 128), i * UNROLL + u, I32)
                    px, py, pz, wx, wy, wz = [take_lanes(v, idx) for v in cols]
                    dx = at[0] - px
                    dy = at[1] - py
                    dz = at[2] - pz
                    sq = jnp.maximum(dx * dx + dy * dy + dz * dz, 1e-30)
                    near = jnp.maximum(1.0 - sq * lax.rsqrt(sq), 0.0)
                    two = near * near
                    phi = two * two * (5.0 - 4.0 * near)
                    acc = [acc[0] + wx * phi, acc[1] + wy * phi, acc[2] + wz * phi]
                return tuple(acc)

            zero = jnp.zeros((8, 128), F32)
            acc = lax.fori_loop(0, turns, step, (zero, zero, zero))
            for c in range(3):
                shift[c, pl.ds(p, 1), :] += jnp.sum(acc[c], axis=0, keepdims=True)

        return page + 1, jnp.max(most)

    lax.while_loop(
        lambda state: state[0] * 128 < state[1], page_body, (jnp.int32(0), jnp.int32(1))
    )

    for c in range(3):
        for jg in range(radial // 8):
            s = shift[c, 8 * jg : 8 * jg + 8, :]
            got = jnp.zeros((8, 128), F32)
            for kg in range(8):
                row = jnp.broadcast_to(s[kg : kg + 1, :], (8, 128))
                got = jnp.where(blocks_of_lanes == kg, take_lanes(row, 16 * sub8 + within), got)
            moved_ref[c, 8 * jg : 8 * jg + 8, :] = base_ref[c, 8 * jg : 8 * jg + 8, :] + got


def metric_kernel(nb, ng, mov_ref, met_ref, allm_ref, allt_ref, halo, sh, rh, sm, rm, st, rt):
    b = lax.axis_index("bulk")
    g = lax.axis_index("grid")
    after = lax.rem(b + 1, nb)
    before = lax.rem(b + nb - 1, nb)
    barrier = pltpu.get_barrier_semaphore()
    for t in (before, after):
        pl.semaphore_signal(barrier, inc=1, device_id=(t, g), device_id_type=MESH)
    for k in range(1, ng):
        pl.semaphore_signal(
            barrier, inc=1, device_id=(b, lax.rem(g + k, ng)), device_id_type=MESH
        )
    pl.semaphore_wait(barrier, 2 + ng - 1)
    halos = [
        pltpu.make_async_remote_copy(
            src_ref=mov_ref,
            dst_ref=halo.at[i],
            send_sem=sh.at[i],
            recv_sem=rh.at[i],
            device_id=(t, g),
            device_id_type=MESH,
        )
        for i, t in enumerate((after, before))
    ]
    for copy in halos:
        copy.start()

    def to_peers(src, dst, ss, rs):
        return [
            pltpu.make_async_remote_copy(
                src_ref=src,
                dst_ref=dst.at[k - 1],
                send_sem=ss.at[k - 1],
                recv_sem=rs.at[k - 1],
                device_id=(b, lax.rem(g + k, ng)),
                device_id_type=MESH,
            )
            for k in range(1, ng)
        ]

    nodes = to_peers(mov_ref, allm_ref, sm, rm)
    for copy in nodes:
        copy.start()
    radial, lines = mov_ref.shape[1:]
    row = iota((radial, lines), 0)
    col = iota((radial, lines), 1)
    dj, dk = [], []
    for c in range(3):
        m = mov_ref[c]
        up, down = pltpu.roll(m, radial - 1, 0), pltpu.roll(m, 1, 0)
        dj.append(
            jnp.where(row == 0, up - m, jnp.where(row == radial - 1, m - down, (up - down) * 0.5))
        )
        up, down = pltpu.roll(m, lines - 1, 1), pltpu.roll(m, 1, 1)
        dk.append(
            jnp.where(col == 0, up - m, jnp.where(col == lines - 1, m - down, (up - down) * 0.5))
        )
    cross = [
        dj[1] * dk[2] - dj[2] * dk[1],
        dj[2] * dk[0] - dj[0] * dk[2],
        dj[0] * dk[1] - dj[1] * dk[0],
    ]
    for copy in halos:
        copy.wait_recv()
    di = [(halo[1, c] - halo[0, c]) * 0.5 for c in range(3)]
    met_ref[...] = di[0] * cross[0] + di[1] * cross[1] + di[2] * cross[2]
    mets = to_peers(met_ref, allt_ref, st, rt)
    for copy in mets:
        copy.start()
    for copy in halos:
        copy.wait_send()
    for copy in nodes + mets:
        copy.wait_send()
        copy.wait_recv()


def blend_kernel(
    don_ref, rec_ref, num_ref, mov_ref, allm_ref, allt_ref, flow_ref, out_ref, rep, tr, acc
):
    radial = mov_ref.shape[1]
    nvar = out_ref.shape[0]
    nrow = num_ref.shape[0]
    sub8 = iota((8, 128), 0)
    for c in range(3):
        tr[c] = jnp.zeros((128, 128), F32)
        tr[c, 0:radial, :] = mov_ref[c]
        tr[c] = tr[c].T

    @pl.loop(0, radial)
    def _(blk):
        idx = jnp.full((128, 128), blk, I32)
        for c in range(3):
            rep[blk, c] = take_lanes(tr[c], idx)

    acc[...] = jnp.zeros(acc.shape, F32)

    @pl.loop(0, nrow)
    def _(r):
        n = num_ref[r, 0]

        @pl.loop(0, (n + ENTRY_UNROLL - 1) // ENTRY_UNROLL)
        def _(i):
            found = []
            for u in range(ENTRY_UNROLL):
                e = i * ENTRY_UNROLL + u
                code = don_ref[r, e]
                recv = rec_ref[r, e]
                k = code // radial
                d = code - k * radial
                sq = None
                for c in range(3):
                    diff = rep[recv, c] - allm_ref[k, c, pl.ds(d, 1), :]
                    sq = diff * diff if sq is None else sq + diff * diff
                w = 1.0 / (0.25 + sq)
                hi = w.astype(BF16)
                lo = (w - hi.astype(F32)).astype(BF16)
                vals = jnp.where(sub8 == nvar, 1.0, jnp.zeros((8, 128), F32))
                met = allt_ref[k, pl.ds(d, 1), :]
                for v in range(nvar):
                    row = met * flow_ref[k, v, pl.ds(d, 1), :]
                    vals = jnp.where(sub8 == v, row, vals)
                vhi = vals.astype(BF16).astype(F32)
                both = jnp.concatenate([vhi, vals - vhi], axis=0).astype(BF16)
                got = lax.dot_general(
                    jnp.concatenate([both, both], axis=1),
                    jnp.concatenate([hi, lo], axis=1),
                    (((1,), (1,)), ((), ())),
                    preferred_element_type=F32,
                )
                got = got[0:8] + got[8:16]
                got = got / got[nvar : nvar + 1, :]
                found.append((recv, jnp.where(e < n, got, 0.0)))
            for recv, got in found:
                first = pl.multiple_of(recv * 8, 8)
                acc[pl.ds(first, 8), :] += got

    for v in range(nvar):
        out_ref[v] = acc[pl.ds(v, radial, stride=8), :]


def local(offsets, flow, control_points, rbf_weights, peer_offset, donor_block, receptor_block):
    _, _, planes, radial, lines = offsets.shape
    nvar = flow.shape[1]
    nb = lax.axis_size("bulk")
    ng = lax.axis_size("grid")
    nd = nb * ng
    grid_here = lax.axis_index("grid")
    plane_ids = lax.axis_index("bulk") * planes + jnp.arange(planes, dtype=I32)
    base = lattice(grid_here[None], plane_ids, planes * nb, radial, lines) + offsets
    base = base.reshape(3, radial, lines)
    rows = control_points.shape[1] // 128
    points = jnp.concatenate([control_points, rbf_weights], axis=0).reshape(6 * rows, 128)
    slots = donor_block.shape[1]
    lrows = -(-slots // 128)
    spare = lrows * 128 - slots

    def lanes(x, fill):
        return jnp.pad(x.reshape(-1), (0, spare), constant_values=fill).reshape(lrows, 128)

    lists = jnp.concatenate(
        [lanes(peer_offset, -1), lanes(donor_block, 0), lanes(receptor_block, 0)], axis=0
    )
    dma = pltpu.SemaphoreType.DMA
    sds = jax.ShapeDtypeStruct
    allp, alll = pl.pallas_call(
        functools.partial(gather_kernel, nb, ng),
        out_shape=(sds((nd, 6 * rows, 128), F32), sds((ng - 1, 3 * lrows, 128), I32)),
        in_specs=[VMEM_SPEC] * 2,
        out_specs=[VMEM_SPEC] * 2,
        scratch_shapes=[dma((nd - 1,)), dma((nd - 1,)), dma((ng - 1,)), dma((ng - 1,))],
        compiler_params=pltpu.CompilerParams(collective_id=0, has_side_effects=True),
        name="gather_points",
    )(points, lists)
    plain = flow.reshape(nvar, radial, lines)
    flows = jnp.stack(
        [
            lax.ppermute(plain, "grid", [(i, (i + k) % ng) for i in range(ng)])
            for k in range(1, ng)
        ]
    )
    nrow = (ng - 1) * lrows
    moved, don, rec, num = pl.pallas_call(
        functools.partial(rbf_kernel, nd, rows, ng, lrows),
        out_shape=(
            sds((3, radial, lines), F32),
            sds((nrow, 128), I32),
            sds((nrow, 128), I32),
            sds((nrow, 128), I32),
        ),
        in_specs=[VMEM_SPEC] * 3,
        out_specs=[VMEM_SPEC] * 4,
        scratch_shapes=[
            pltpu.VMEM((6, nd * rows, 128), F32),
            pltpu.VMEM((6, 128, 128), F32),
            pltpu.VMEM((3, radial, 128), F32),
            pltpu.VMEM((6, radial, 8, 128), F32),
            pltpu.VMEM((6, radial * 8, 128), F32),
            pltpu.VMEM((radial * 8, 128), I32),
            pltpu.VMEM((radial, 128), I32),
            pltpu.SMEM((radial, 128), I32),
            pltpu.VMEM((3, radial, 128), F32),
            pltpu.VMEM((3, nrow, 128), I32),
            dma,
        ],
        cost_estimate=pl.CostEstimate(flops=200000000, bytes_accessed=500000, transcendentals=0),
        name="move_nodes",
    )(base, allp, alll)
    metric, allm, allt = pl.pallas_call(
        functools.partial(metric_kernel, nb, ng),
        out_shape=(
            sds((radial, lines), F32),
            sds((ng - 1, 3, radial, lines), F32),
            sds((ng - 1, radial, lines), F32),
        ),
        in_specs=[VMEM_SPEC],
        out_specs=[VMEM_SPEC] * 3,
        scratch_shapes=[
            pltpu.VMEM((2, 3, radial, lines), F32),
            dma((2,)),
            dma((2,)),
            dma((ng - 1,)),
            dma((ng - 1,)),
            dma((ng - 1,)),
            dma((ng - 1,)),
        ],
        compiler_params=pltpu.CompilerParams(collective_id=1, has_side_effects=True),
        name="metric",
    )(moved)
    fringe = pl.pallas_call(
        blend_kernel,
        out_shape=sds((nvar, radial, lines), F32),
        in_specs=[SMEM_SPEC] * 3 + [VMEM_SPEC] * 4,
        out_specs=VMEM_SPEC,
        scratch_shapes=[
            pltpu.VMEM((radial, 3, 128, 128), F32),
            pltpu.VMEM((3, 128, 128), F32),
            pltpu.VMEM((radial * 8, 128), F32),
        ],
        name="blend",
    )(don, rec, num, moved, allm, allt, flows)
    return (
        moved.reshape(1, 3, planes, radial, lines),
        metric.reshape(1, planes, radial, lines),
        fringe.reshape(1, nvar, planes, radial, lines),
    )


def solution(mesh):
    in_specs = (
        P("grid", None, "bulk", None, None),
        P("grid", None, "bulk", None, None),
        P(None, ("bulk", "grid")),
        P(None, ("bulk", "grid")),
        P("grid", "bulk", None),
        P("grid", "bulk"),
        P("grid", "bulk"),
    )
    out_specs = (
        P("grid", None, "bulk", None, None),
        P("grid", "bulk", None, None),
        P("grid", None, "bulk", None, None),
    )
    return jax.shard_map(local, mesh=mesh, in_specs=in_specs, out_specs=out_specs, check_vma=False)
```

time: 535 us -> 107 us (0.20)
  matrix products: 339 us -> 0 us
  blocking collectives: 136 us -> 0 us
  Pallas kernels: 0 us -> 79 us
  other arithmetic: 22.2 us -> 1.34 us
  waiting for transfers between devices: 22.7 us -> 11.2 us
    dot_general x21 -> x0, matrix products: 339 us -> none  [the longest x8 299 us: kernel_sum(): return jnp.einsum('ck,nk->cn', weights, basis, precision=HIGHEST)]
    all_gather x2 -> x0, blocking collectives: 136 us -> none  [the longest x1 71.5 us: local(): lax.all_gather(control_points, ('bulk', 'grid'), axis=1, tiled=True)]
    pallas_call x0 -> x4, Pallas kernels: none -> 79 us  [the longest x1 24.1 us: local(): pl.pallas_call(blend_kernel, out_shape=sds((nvar, radial, lines), F32), i...]
    all_to_all x2 -> x0, waiting for transfers between devices: 22.7 us -> none  [the longest x1 19.4 us: local(): lax.all_to_all(sent, 'grid', split_axis=0, concat_axis=0, tiled=True)]
    reduce_sum x9 -> x0, other arithmetic: 19.6 us -> none  [the longest x8 19.5 us: blend(): totals = jnp.sum(weight, axis=2)]
    ppermute x2 -> x7, waiting for transfers between devices: 0.01 us -> 11.2 us  [local(): lax.ppermute(plain, 'grid', [(i, (i + k) % ng) for i in range(ng)])]
    ppermute x2 -> x7, starting transfers between devices: 1.79 us -> 11.9 us  [local(): lax.ppermute(plain, 'grid', [(i, (i + k) % ng) for i in range(ng)])]
    all_to_all x2 -> x0, starting transfers between devices: 7.04 us -> none  [the longest x1 3.55 us: local(): lax.all_to_all(sent, 'grid', split_axis=0, concat_axis=0, tiled=True)]
  transfers between devices with their start and end apart: 4 -> 7, of which waited for: 2 -> 2; matrix products, arithmetic and copies ran while one was open for 1% -> 2% of each run, Pallas kernels for 0% -> 51%
where the time goes in v1:
time: 107 us; the launch traced here: 108 us
  Pallas kernels  79 us (74%)
  starting transfers between devices  11.9 us (11%)
  waiting for transfers between devices  11.2 us (10%)
  local copies, waits for them, and re-layouts  3.38 us (3%)
  other arithmetic  1.34 us (1%)
    pallas_call x1, Pallas kernels, local(): pl.pallas_call(blend_kernel, out_shape=sds((nvar, radial, lines), F32), i...  24.1 us
    pallas_call x1, Pallas kernels, local(): pl.pallas_call(functools.partial(rbf_kernel, nd, rows, ng, lrows), out_sh...  23.8 us
    pallas_call x1, Pallas kernels, local(): pl.pallas_call(functools.partial(gather_kernel, nb, ng), out_shape=(sds((...  17 us
    pallas_call x1, Pallas kernels, local(): pl.pallas_call(functools.partial(metric_kernel, nb, ng), out_shape=(sds((...  14.2 us
    ppermute x7, starting transfers between devices, local(): lax.ppermute(plain, 'grid', [(i, (i + k) % ng) for i in range(ng)])  11.9 us
    ppermute x7, waiting for transfers between devices, local(): lax.ppermute(plain, 'grid', [(i, (i + k) % ng) for i in range(ng)])  11.2 us
    unnamed x25, local copies, waits for them, and re-layouts  2.76 us
  transfers between devices with their start and end apart: 7, of which 2 were waited for; matrix products, arithmetic and copies ran while one was open for 2% of the time, Pallas kernels for 51%

profile of v1, /device:TPU:0, one launch (start us, length us, event | category | flops | bytes accessed | tf_op | source)
XLA Modules:
  0.0 107.8 jit_solution(16316847028241503707)
XLA Ops:
  0.6 6.1 %collective-permute-start.6 = (f32[5,24,128]{2,1,0:T(8,128)}, f32[5,24,128]{2,1,0:T(8,128)S(1)}, u32[]{:S(2)}, u32[]{:S(2)}) collective-permute-start(f32[5,24,128]{2,1,0:T(8,128)} %bitcast.41), channel_id=1, source_target_pairs={{0,7},{1,0},{2,1},{3,2},{4,3},{5,4},{6,5},{7,6},{8,15},{9,8},{10,9... | collective-permute-start | bytes 184328 | tf_op jit(solution)/shard_map/ppermute | solution.py:469
  6.7 0.4 collective-permute-start.5
  7.2 3.0 %collective-permute-start.3 = (f32[5,24,128]{2,1,0:T(8,128)}, f32[5,24,128]{2,1,0:T(8,128)S(1)}, u32[]{:S(2)}, u32[]{:S(2)}) collective-permute-start(f32[5,24,128]{2,1,0:T(8,128)} %bitcast.44), channel_id=1, source_target_pairs={{0,4},{1,5},{2,6},{3,7},{4,0},{5,1},{6,2},{7,3},{8,12},{9,13},{10,... | collective-permute-start | bytes 184328 | tf_op jit(solution)/shard_map/ppermute | solution.py:469
  10.1 1.5 %collective-permute-start = (f32[5,24,128]{2,1,0:T(8,128)}, f32[5,24,128]{2,1,0:T(8,128)S(1)}, u32[]{:S(2)}, u32[]{:S(2)}) collective-permute-start(f32[5,24,128]{2,1,0:T(8,128)} %bitcast.45), channel_id=1, source_target_pairs={{0,1},{1,2},{2,3},{3,4},{4,5},{5,6},{6,7},{7,0},{8,9},{9,10},{10,1... | collective-permute-start | bytes 184328 | tf_op jit(solution)/shard_map/ppermute | solution.py:469
  11.9 0.0 copy-start.5
  11.9 0.0 copy-start.7
  11.9 0.0 copy-start.6
  11.9 0.0 copy-start.4
  11.9 0.0 copy-start.3
  11.9 0.6 copy-done.5
  12.5 0.0 copy-done.7
  12.6 0.0 copy-done.6
  12.6 0.0 copy-done.4
  12.6 0.0 copy-done.3
  12.7 0.1 broadcast_add_fusion
  12.7 0.7 copy-done.1
  13.4 0.6 fusion.base_ref
  14.0 0.6 pad_add_fusion.lst_ref
  14.6 0.6 reshape.222.pts_ref
  15.2 17.0 %gather_points.1 = (f32[32,24,128]{2,1,0:T(8,128)}, s32[7,6,128]{2,1,0:T(8,128)}) custom-call(f32[24,128]{1,0:T(8,128)} %reshape.222.pts_ref, s32[6,128]{1,0:T(8,128)} %pad_add_fusion.lst_ref), custom_call_target="tpu_custom_call" | custom-call | tf_op jit(solution)/shard_map/gather_points/pallas_call | solution.py:457
  32.2 0.0 copy-start.8
  32.2 23.8 %move_nodes.1 = (f32[3,24,128]{2,1,0:T(8,128)}, s32[14,128]{1,0:T(8,128)}, s32[14,128]{1,0:T(8,128)}, s32[14,128]{1,0:T(8,128)}) custom-call(f32[3,24,128]{2,1,0:T(8,128)} %fusion.base_ref, f32[32,24,128]{2,1,0:T(8,128)} %get-tuple-element.12.pts_ref, s32[7,6,128]{2,1,0:T(8,128)} %get-tuple-element.13.lst_ref), custom_call_target="tpu_custom_call" | custom-call | flops 200000000 | bytes 500000 | tf_op jit(solution)/shard_map/move_nodes/pallas_call | solution.py:474
  56.0 14.2 %metric.1 = (f32[24,128]{1,0:T(8,128)}, f32[7,3,24,128]{3,2,1,0:T(8,128)}, f32[7,24,128]{2,1,0:T(8,128)}) custom-call(f32[3,24,128]{2,1,0:T(8,128)} %get-tuple-element.14.mov_ref), custom_call_target="tpu_custom_call" | custom-call | tf_op jit(solution)/shard_map/metric/pallas_call | solution.py:500
  70.2 0.0 collective-permute-done
  70.2 0.9 collective-permute-start.1
  71.1 5.2 %collective-permute-done.1 = f32[5,24,128]{2,1,0:T(8,128)S(1)} collective-permute-done((f32[5,24,128]{2,1,0:T(8,128)S(1)}, f32[5,24,128]{2,1,0:T(8,128)S(1)}, u32[]{:S(2)}, u32[]{:S(2)}) %collective-permute-start.1) | collective-permute-done | bytes 61472 | tf_op jit(solution)/shard_map/ppermute | solution.py:469
  76.3 6.0 %collective-permute-done.2 = f32[5,24,128]{2,1,0:T(8,128)S(1)} collective-permute-done((f32[5,24,128]{2,1,0:T(8,128)S(1)}, f32[5,24,128]{2,1,0:T(8,128)S(1)}, u32[]{:S(2)}, u32[]{:S(2)}) %collective-permute-start.2) | collective-permute-done | bytes 61472 | tf_op jit(solution)/shard_map/ppermute | solution.py:469
  82.3 0.0 collective-permute-done.3
  82.3 0.0 collective-permute-done.4
  82.4 0.7 copy-done
  83.2 24.1 %blend.1 = f32[5,24,128]{2,1,0:T(8,128)} custom-call(s32[14,128]{1,0:T(8,128)} %get-tuple-element.16.don_ref, s32[14,128]{1,0:T(8,128)} %get-tuple-element.17.rec_ref, s32[14,128]{1,0:T(8,128)} %get-tuple-element.18.num_ref, f32[3,24,128]{2,1,0:T(8,128)} %get-tuple-element.14.mov_ref, f32[7,3,24,128]{3,2,1,0:T(8,128)} %get-tuple-element.19.allm_ref, ...), custom_call_target="tpu_custom_call" | custom-call | tf_op jit(solution)/shard_map/blend/pallas_call | solution.py:521
  107.2 0.6 copy.20
  (23 shorter events, 0.1 us)
Async XLA Ops:
  0.6 81.8 %collective-permute-start.6 = (f32[5,24,128]{2,1,0:T(8,128)}, f32[5,24,128]{2,1,0:T(8,128)S(1)}, u32[]{:S(2)}, u32[]{:S(2)}) collective-permute-start(f32[5,24,128]{2,1,0:T(8,128)} %bitcast.41), channel_id=1, source_target_pairs={{0,7},{1,0},{2,1},{3,2},{4,3},{5,4},{6,5},{7,6},{8,15},{9,8},{10,9... | collective-permute-start | bytes 184328 | tf_op jit(solution)/shard_map/ppermute | solution.py:469
  6.7 75.7 %collective-permute-start.5 = (f32[5,24,128]{2,1,0:T(8,128)}, f32[5,24,128]{2,1,0:T(8,128)S(1)}, u32[]{:S(2)}, u32[]{:S(2)}) collective-permute-start(f32[5,24,128]{2,1,0:T(8,128)} %bitcast.42), channel_id=1, source_target_pairs={{0,6},{1,7},{2,0},{3,1},{4,2},{5,3},{6,4},{7,5},{8,14},{9,15},{10,... | collective-permute-start | bytes 184328 | tf_op jit(solution)/shard_map/ppermute | solution.py:469
  7.2 75.2 %collective-permute-start.4 = (f32[5,24,128]{2,1,0:T(8,128)}, f32[5,24,128]{2,1,0:T(8,128)S(1)}, u32[]{:S(2)}, u32[]{:S(2)}) collective-permute-start(f32[5,24,128]{2,1,0:T(8,128)} %bitcast.43), channel_id=1, source_target_pairs={{0,5},{1,6},{2,7},{3,0},{4,1},{5,2},{6,3},{7,4},{8,13},{9,14},{10,... | collective-permute-start | bytes 184328 | tf_op jit(solution)/shard_map/ppermute | solution.py:469
  7.2 75.2 %collective-permute-start.3 = (f32[5,24,128]{2,1,0:T(8,128)}, f32[5,24,128]{2,1,0:T(8,128)S(1)}, u32[]{:S(2)}, u32[]{:S(2)}) collective-permute-start(f32[5,24,128]{2,1,0:T(8,128)} %bitcast.44), channel_id=1, source_target_pairs={{0,4},{1,5},{2,6},{3,7},{4,0},{5,1},{6,2},{7,3},{8,12},{9,13},{10,... | collective-permute-start | bytes 184328 | tf_op jit(solution)/shard_map/ppermute | solution.py:469
  10.1 60.1 %collective-permute-start = (f32[5,24,128]{2,1,0:T(8,128)}, f32[5,24,128]{2,1,0:T(8,128)S(1)}, u32[]{:S(2)}, u32[]{:S(2)}) collective-permute-start(f32[5,24,128]{2,1,0:T(8,128)} %bitcast.45), channel_id=1, source_target_pairs={{0,1},{1,2},{2,3},{3,4},{4,5},{5,6},{6,7},{7,0},{8,9},{9,10},{10,1... | collective-permute-start | bytes 184328 | tf_op jit(solution)/shard_map/ppermute | solution.py:469
  11.9 0.7 copy-start.5
  11.9 0.7 copy-start.7
  11.9 0.7 copy-start.6
  11.9 0.7 copy-start.4
  11.9 0.7 copy-start.3
  12.6 0.8 copy-start.1
  32.2 38.0 %copy-start.8 = (f32[1,5,1,24,128]{4,3,2,1,0:T(8,128)S(1)}, f32[1,5,1,24,128]{4,3,2,1,0:T(8,128)}, u32[]{:S(2)}) copy-start(f32[1,5,1,24,128]{4,3,2,1,0:T(8,128)} %param.8) | copy-start | bytes 184324
  70.2 6.1 %collective-permute-start.1 = (f32[5,24,128]{2,1,0:T(8,128)S(1)}, f32[5,24,128]{2,1,0:T(8,128)S(1)}, u32[]{:S(2)}, u32[]{:S(2)}) collective-permute-start(f32[5,24,128]{2,1,0:T(8,128)S(1)} %bitcast.46), channel_id=1, source_target_pairs={{0,2},{1,3},{2,4},{3,5},{4,6},{5,7},{6,0},{7,1},{8,10},{9,11},{10,... | collective-permute-start | bytes 184328 | tf_op jit(solution)/shard_map/ppermute | solution.py:469
  76.3 6.0 %collective-permute-start.2 = (f32[5,24,128]{2,1,0:T(8,128)S(1)}, f32[5,24,128]{2,1,0:T(8,128)S(1)}, u32[]{:S(2)}, u32[]{:S(2)}) collective-permute-start(f32[5,24,128]{2,1,0:T(8,128)S(1)} %bitcast.47), channel_id=1, source_target_pairs={{0,3},{1,4},{2,5},{3,6},{4,7},{5,0},{6,1},{7,2},{8,11},{9,12},{10,... | collective-permute-start | bytes 184328 | tf_op jit(solution)/shard_map/ppermute | solution.py:469
  82.4 0.8 copy-start
  83.2 24.1 %copy-start.2 = (f32[24,128]{1,0:T(8,128)S(1)}, f32[24,128]{1,0:T(8,128)}, u32[]{:S(2)}) copy-start(f32[24,128]{1,0:T(8,128)} %get-tuple-element.15) | copy-start | bytes 36868

commit v2 on v1

--- a/solution.py
+++ b/solution.py
@@ -13,7 +13,7 @@
 CULL = SUPPORT * SUPPORT * 1.0001
 FAR = 1.0e9
 UNROLL = 16
-ENTRY_UNROLL = 2
+ENTRY_UNROLL = 4
 F32 = jnp.float32
 I32 = jnp.int32
 BF16 = jnp.bfloat16
@@ -65,64 +65,106 @@
     return pos
 
 
-def gather_kernel(nb, ng, pts_ref, lst_ref, allp_ref, alll_ref, sp, rp, sl, rl):
+def halves(n):
+    return (n // 2, 2) if n % 2 == 0 else (n, 1)
+
+
+def line_and_pair(me, n):
+    high, low = halves(n)
+    place = lax.rem(me, low)
+    line = [lax.rem(me // low + m, high) * low + place for m in range(1, high)]
+    pair = [me + 1 - 2 * place] if low == 2 else []
+    return line, pair
+
+
+def gather_kernel(
+    nb, ng, pts_ref, lst_ref, flow_ref, allp_ref, alll_ref, allf_ref, sp, rp, sl, rl, sf, rf
+):
     b = lax.axis_index("bulk")
     g = lax.axis_index("grid")
-    nd = nb * ng
-    me = b * ng + g
+    gline, gpair = line_and_pair(g, ng)
+    bline, bpair = line_and_pair(b, nb)
     barrier = pltpu.get_barrier_semaphore()
-
-    def peer_of(k):
-        peer = lax.rem(me + k, nd)
-        return (peer // ng, lax.rem(peer, ng))
-
-    @pl.loop(1, nd)
-    def _(k):
-        pl.semaphore_signal(barrier, inc=1, device_id=peer_of(k), device_id_type=MESH)
-
-    pl.semaphore_wait(barrier, nd - 1)
-
-    def points_copy(k, slot):
-        return pltpu.make_async_remote_copy(
-            src_ref=pts_ref,
-            dst_ref=allp_ref.at[slot],
-            send_sem=sp.at[k - 1],
-            recv_sem=rp.at[k - 1],
-            device_id=peer_of(k),
+    peers = [(b, t) for t in gline + gpair] + [(t, g) for t in bline + bpair]
+    for peer in peers:
+        pl.semaphore_signal(barrier, inc=1, device_id=peer, device_id_type=MESH)
+    pl.semaphore_wait(barrier, len(peers))
+    sent = {"p": [], "l": [], "f": []}
+
+    def send(kind, slot, peer, own):
+        source, full, ss, rs = {
+            "p": (pts_ref, allp_ref, sp, rp),
+            "l": (lst_ref, alll_ref, sl, rl),
+            "f": (flow_ref, allf_ref, sf, rf),
+        }[kind]
+        copy = pltpu.make_async_remote_copy(
+            src_ref=source if own else full.at[slot],
+            dst_ref=full.at[slot],
+            send_sem=ss.at[len(sent[kind])],
+            recv_sem=rs.at[slot],
+            device_id=peer,
             device_id_type=MESH,
         )
-
-    def list_copy(k):
-        return pltpu.make_async_remote_copy(
-            src_ref=lst_ref,
-            dst_ref=alll_ref.at[k - 1],
-            send_sem=sl.at[k - 1],
-            recv_sem=rl.at[k - 1],
-            device_id=(b, lax.rem(g + k, ng)),
+        copy.start()
+        sent[kind].append(copy)
+
+    def arrived(kind, slot):
+        full, ss, rs = {
+            "p": (allp_ref, sp, rp),
+            "l": (alll_ref, sl, rl),
+            "f": (allf_ref, sf, rf),
+        }[kind]
+        pltpu.make_async_remote_copy(
+            src_ref=full.at[slot],
+            dst_ref=full.at[slot],
+            send_sem=ss.at[0],
+            recv_sem=rs.at[slot],
+            device_id=peers[0],
             device_id_type=MESH,
-        )
-
-    @pl.loop(1, nd)
-    def _(k):
-        points_copy(k, me).start()
-
-    @pl.loop(1, ng)
-    def _(k):
-        list_copy(k).start()
-
-    allp_ref[me] = pts_ref[...]
-
-    @pl.loop(1, nd)
-    def _(k):
-        copy = points_copy(k, lax.rem(me + nd - k, nd))
-        copy.wait_send()
-        copy.wait_recv()
-
-    @pl.loop(1, ng)
-    def _(k):
-        copy = list_copy(k)
-        copy.wait_send()
-        copy.wait_recv()
+        ).wait_recv()
+
+    def across(s, own):
+        for t in bline + bpair:
+            send("p", b * ng + s, (t, g), own)
+
+    for t in gline + gpair:
+        send("p", b * ng + g, (b, t), True)
+    across(g, True)
+    for kind in ("l", "f"):
+        for t in gline + gpair:
+            send(kind, g, (b, t), True)
+    allp_ref[b * ng + g] = pts_ref[...]
+    alll_ref[g] = lst_ref[...]
+    for s in gline:
+        arrived("p", b * ng + s)
+        for t in gpair:
+            send("p", b * ng + s, (b, t), False)
+        across(s, False)
+    for s in gline:
+        for kind in ("l", "f"):
+            arrived(kind, s)
+            for t in gpair:
+                send(kind, s, (b, t), False)
+    low = halves(ng)[1]
+    other = gpair + [t + gpair[0] - g for t in gline] if low == 2 else []
+    for s in other:
+        arrived("p", b * ng + s)
+        across(s, False)
+    for x in bline:
+        for s in [g] + gline + other:
+            arrived("p", x * ng + s)
+            for t in bpair:
+                send("p", x * ng + s, (t, g), False)
+    for t in bpair:
+        for x in [t] + [u + t - b for u in bline]:
+            for s in [g] + gline + other:
+                arrived("p", x * ng + s)
+    for s in other:
+        arrived("l", s)
+        arrived("f", s)
+    for kind in sent:
+        for copy in sent[kind]:
+            copy.wait_send()
 
 
 def rbf_kernel(
@@ -130,6 +172,7 @@
     rows,
     ng,
     lrows,
+    here_ref,
     base_ref,
     pts_ref,
     lst_ref,
@@ -162,12 +205,14 @@
             mask.astype(F32).astype(BF16), upper, preferred_element_type=F32
         ).astype(I32)
 
-    nrow = (ng - 1) * lrows
-    for k in range(ng - 1):
+    nrow = ng * lrows
+    for k in range(ng):
         for c in range(3):
             names[c, k * lrows : (k + 1) * lrows, :] = lst_ref[k, c * lrows : (c + 1) * lrows, :]
     owner = iota((nrow, 128), 0) // lrows
-    counts = running(names[0] == owner)
+    target = owner + 1 + names[0]
+    target = jnp.where(target >= ng, target - ng, target)
+    counts = running(target == here_ref[0])
     pos = search(counts, iota((nrow, 128), 1))
     don_ref[...] = owner * radial + take_lanes(names[1], pos)
     rec_ref[...] = take_lanes(names[2], pos)
@@ -296,13 +341,11 @@
     after = lax.rem(b + 1, nb)
     before = lax.rem(b + nb - 1, nb)
     barrier = pltpu.get_barrier_semaphore()
-    for t in (before, after):
-        pl.semaphore_signal(barrier, inc=1, device_id=(t, g), device_id_type=MESH)
-    for k in range(1, ng):
-        pl.semaphore_signal(
-            barrier, inc=1, device_id=(b, lax.rem(g + k, ng)), device_id_type=MESH
-        )
-    pl.semaphore_wait(barrier, 2 + ng - 1)
+    gline, gpair = line_and_pair(g, ng)
+    peers = [(before, g), (after, g)] + [(b, t) for t in gline + gpair]
+    for peer in peers:
+        pl.semaphore_signal(barrier, inc=1, device_id=peer, device_id_type=MESH)
+    pl.semaphore_wait(barrier, len(peers))
     halos = [
         pltpu.make_async_remote_copy(
             src_ref=mov_ref,
@@ -317,22 +360,29 @@
     for copy in halos:
         copy.start()
 
-    def to_peers(src, dst, ss, rs):
-        return [
-            pltpu.make_async_remote_copy(
-                src_ref=src,
-                dst_ref=dst.at[k - 1],
-                send_sem=ss.at[k - 1],
-                recv_sem=rs.at[k - 1],
-                device_id=(b, lax.rem(g + k, ng)),
-                device_id_type=MESH,
-            )
-            for k in range(1, ng)
-        ]
-
-    nodes = to_peers(mov_ref, allm_ref, sm, rm)
-    for copy in nodes:
+    sent = {"m": [], "t": []}
+
+    def describe(kind, slot, peer, own, n):
+        source, full, ss, rs = {
+            "m": (mov_ref, allm_ref, sm, rm),
+            "t": (met_ref, allt_ref, st, rt),
+        }[kind]
+        return pltpu.make_async_remote_copy(
+            src_ref=source if own else full.at[slot],
+            dst_ref=full.at[slot],
+            send_sem=ss.at[n],
+            recv_sem=rs.at[slot],
+            device_id=peer,
+            device_id_type=MESH,
+        )
+
+    def send(kind, slot, peer, own):
+        copy = describe(kind, slot, peer, own, len(sent[kind]))
         copy.start()
+        sent[kind].append(copy)
+
+    for t in gline + gpair:
+        send("m", g, (b, t), True)
     radial, lines = mov_ref.shape[1:]
     row = iota((radial, lines), 0)
     col = iota((radial, lines), 1)
@@ -356,14 +406,19 @@
         copy.wait_recv()
     di = [(halo[1, c] - halo[0, c]) * 0.5 for c in range(3)]
     met_ref[...] = di[0] * cross[0] + di[1] * cross[1] + di[2] * cross[2]
-    mets = to_peers(met_ref, allt_ref, st, rt)
-    for copy in mets:
-        copy.start()
-    for copy in halos:
+    for t in gline + gpair:
+        send("t", g, (b, t), True)
+    for kind in ("m", "t"):
+        for s in gline:
+            describe(kind, s, peers[0], False, 0).wait_recv()
+            for t in gpair:
+                send(kind, s, (b, t), False)
+    other = gpair + [t + gpair[0] - g for t in gline] if gpair else []
+    for kind in ("m", "t"):
+        for s in other:
+            describe(kind, s, peers[0], False, 0).wait_recv()
+    for copy in halos + sent["m"] + sent["t"]:
         copy.wait_send()
-    for copy in nodes + mets:
-        copy.wait_send()
-        copy.wait_recv()
 
 
 def blend_kernel(
@@ -450,27 +505,25 @@
         return jnp.pad(x.reshape(-1), (0, spare), constant_values=fill).reshape(lrows, 128)
 
     lists = jnp.concatenate(
-        [lanes(peer_offset, -1), lanes(donor_block, 0), lanes(receptor_block, 0)], axis=0
+        [lanes(peer_offset, -4 * ng), lanes(donor_block, 0), lanes(receptor_block, 0)], axis=0
     )
     dma = pltpu.SemaphoreType.DMA
     sds = jax.ShapeDtypeStruct
-    allp, alll = pl.pallas_call(
+    many = nd + ng
+    allp, alll, allf = pl.pallas_call(
         functools.partial(gather_kernel, nb, ng),
-        out_shape=(sds((nd, 6 * rows, 128), F32), sds((ng - 1, 3 * lrows, 128), I32)),
-        in_specs=[VMEM_SPEC] * 2,
-        out_specs=[VMEM_SPEC] * 2,
-        scratch_shapes=[dma((nd - 1,)), dma((nd - 1,)), dma((ng - 1,)), dma((ng - 1,))],
+        out_shape=(
+            sds((nd, 6 * rows, 128), F32),
+            sds((ng, 3 * lrows, 128), I32),
+            sds((ng, nvar, radial, lines), F32),
+        ),
+        in_specs=[VMEM_SPEC] * 3,
+        out_specs=[VMEM_SPEC] * 3,
+        scratch_shapes=[dma((many * 2,)), dma((nd,)), dma((many,)), dma((ng,)), dma((many,)), dma((ng,))],
         compiler_params=pltpu.CompilerParams(collective_id=0, has_side_effects=True),
         name="gather_points",
-    )(points, lists)
-    plain = flow.reshape(nvar, radial, lines)
-    flows = jnp.stack(
-        [
-            lax.ppermute(plain, "grid", [(i, (i + k) % ng) for i in range(ng)])
-            for k in range(1, ng)
-        ]
-    )
-    nrow = (ng - 1) * lrows
+    )(points, lists, flow.reshape(nvar, radial, lines))
+    nrow = ng * lrows
     moved, don, rec, num = pl.pallas_call(
         functools.partial(rbf_kernel, nd, rows, ng, lrows),
         out_shape=(
@@ -479,7 +532,7 @@
             sds((nrow, 128), I32),
             sds((nrow, 128), I32),
         ),
-        in_specs=[VMEM_SPEC] * 3,
+        in_specs=[SMEM_SPEC] + [VMEM_SPEC] * 3,
         out_specs=[VMEM_SPEC] * 4,
         scratch_shapes=[
             pltpu.VMEM((6, nd * rows, 128), F32),
@@ -496,13 +549,13 @@
         ],
         cost_estimate=pl.CostEstimate(flops=200000000, bytes_accessed=500000, transcendentals=0),
         name="move_nodes",
-    )(base, allp, alll)
+    )(grid_here.reshape(1).astype(I32), base, allp, alll)
     metric, allm, allt = pl.pallas_call(
         functools.partial(metric_kernel, nb, ng),
         out_shape=(
             sds((radial, lines), F32),
-            sds((ng - 1, 3, radial, lines), F32),
-            sds((ng - 1, radial, lines), F32),
+            sds((ng, 3, radial, lines), F32),
+            sds((ng, radial, lines), F32),
         ),
         in_specs=[VMEM_SPEC],
         out_specs=[VMEM_SPEC] * 3,
@@ -510,10 +563,10 @@
             pltpu.VMEM((2, 3, radial, lines), F32),
             dma((2,)),
             dma((2,)),
-            dma((ng - 1,)),
-            dma((ng - 1,)),
-            dma((ng - 1,)),
-            dma((ng - 1,)),
+            dma((2 * ng,)),
+            dma((ng,)),
+            dma((2 * ng,)),
+            dma((ng,)),
         ],
         compiler_params=pltpu.CompilerParams(collective_id=1, has_side_effects=True),
         name="metric",
@@ -529,7 +582,7 @@
             pltpu.VMEM((radial * 8, 128), F32),
         ],
         name="blend",
-    )(don, rec, num, moved, allm, allt, flows)
+    )(don, rec, num, moved, allm, allt, allf)
     return (
         moved.reshape(1, 3, planes, radial, lines),
         metric.reshape(1, planes, radial, lines),

time: 107 us -> 81.3 us (0.76); the launches traced: 108 us -> 80.1 us
  starting transfers between devices: 11.9 us -> 0 us
  waiting for transfers between devices: 11.2 us -> 0 us
  Pallas kernels: 79 us -> 74.8 us
    ppermute x7 -> x0, starting transfers between devices: 11.9 us -> none  [local(): lax.ppermute(plain, 'grid', [(i, (i + k) % ng) for i in range(ng)])]
    ppermute x7 -> x0, waiting for transfers between devices: 11.2 us -> none  [local(): lax.ppermute(plain, 'grid', [(i, (i + k) % ng) for i in range(ng)])]
    pallas_call x1, Pallas kernels: 24.1 us -> 18.5 us  [local(): pl.pallas_call(blend_kernel, out_shape=sds((nvar, radial, lines), F32), i...]
    pallas_call x1, Pallas kernels: 17 us -> 20.8 us  [local(): pl.pallas_call(functools.partial(gather_kernel, nb, ng), out_shape=(sds((...]
    pallas_call x1, Pallas kernels: 14.2 us -> 11 us  [local(): pl.pallas_call(functools.partial(metric_kernel, nb, ng), out_shape=(sds((...]
    unnamed x25 -> x15, local copies, waits for them, and re-layouts: 2.76 us -> 2.55 us
  transfers between devices with their start and end apart: 7 -> 0, of which waited for: 2 -> 0; matrix products, arithmetic and copies ran while one was open for 2% -> 0% of each run, Pallas kernels for 51% -> 0%
where the time goes in v2:
time: 81.3 us; the launch traced here: 80.1 us
  Pallas kernels  74.8 us (92%)
  local copies, waits for them, and re-layouts  3.16 us (4%)
  other arithmetic  1.33 us (2%)
  between operations  0.88 us (1%)
    pallas_call x1, Pallas kernels, local(): pl.pallas_call(functools.partial(rbf_kernel, nd, rows, ng, lrows), out_sh...  24.5 us
    pallas_call x1, Pallas kernels, local(): pl.pallas_call(functools.partial(gather_kernel, nb, ng), out_shape=(sds((...  20.8 us
    pallas_call x1, Pallas kernels, local(): pl.pallas_call(blend_kernel, out_shape=sds((nvar, radial, lines), F32), i...  18.5 us
    pallas_call x1, Pallas kernels, local(): pl.pallas_call(functools.partial(metric_kernel, nb, ng), out_shape=(sds((...  11 us
    unnamed x15, local copies, waits for them, and re-layouts  2.55 us

profile of v2, /device:TPU:0, one launch (start us, length us, event | category | flops | bytes accessed | tf_op | source)
XLA Modules:
  0.0 80.1 jit_solution(16623716902746083001)
XLA Ops:
  0.6 0.0 copy-start
  0.9 0.1 broadcast_add_fusion
  0.9 0.5 copy-done
  1.4 0.0 copy-start.2
  1.4 0.0 copy-start.3
  1.4 0.6 fusion.base_ref
  2.0 0.1 copy-done.2
  2.1 0.0 copy-done.3
  2.2 0.0 copy-start.6
  2.2 0.6 reshape.219.pts_ref
  2.8 0.0 copy-start.5
  2.8 0.1 copy-done.6
  2.8 0.6 copy-done.5
  3.4 0.0 copy-start.4
  3.4 0.7 copy-done.4
  4.1 0.6 pad_add_fusion.lst_ref
  4.7 20.8 %gather_points.1 = (f32[32,24,128]{2,1,0:T(8,128)}, s32[8,6,128]{2,1,0:T(8,128)}, f32[8,5,24,128]{3,2,1,0:T(8,128)}) custom-call(f32[24,128]{1,0:T(8,128)} %reshape.219.pts_ref, s32[6,128]{1,0:T(8,128)} %pad_add_fusion.lst_ref, f32[5,24,128]{2,1,0:T(8,128)} %bitcast.25), custom_call_target="tpu_custom_call" | custom-call | tf_op jit(solution)/shard_map/gather_points/pallas_call | solution.py:513
  25.5 24.5 %move_nodes.1 = (f32[3,24,128]{2,1,0:T(8,128)}, s32[16,128]{1,0:T(8,128)}, s32[16,128]{1,0:T(8,128)}, s32[16,128]{1,0:T(8,128)}) custom-call(s32[1]{0:T(128)} %bitcast.here_ref, f32[3,24,128]{2,1,0:T(8,128)} %fusion.base_ref, f32[32,24,128]{2,1,0:T(8,128)} %get-tuple-element.13.pts_ref, s32[8,6,128]{2,1,0:T(8,128)} %get-tuple-element.14.lst_ref), custom_call_target="tpu_custom_call" | custom-call | flops 200000000 | bytes 500000 | tf_op jit(solution)/shard_map/move_nodes/pallas_call | solution.py:527
  50.0 11.0 %metric.1 = (f32[24,128]{1,0:T(8,128)}, f32[8,3,24,128]{3,2,1,0:T(8,128)}, f32[8,24,128]{2,1,0:T(8,128)}) custom-call(f32[3,24,128]{2,1,0:T(8,128)} %get-tuple-element.15.mov_ref), custom_call_target="tpu_custom_call" | custom-call | tf_op jit(solution)/shard_map/metric/pallas_call | solution.py:553
  61.0 0.0 copy-start.1
  61.1 18.5 %blend.1 = f32[5,24,128]{2,1,0:T(8,128)} custom-call(s32[16,128]{1,0:T(8,128)} %get-tuple-element.17.don_ref, s32[16,128]{1,0:T(8,128)} %get-tuple-element.18.rec_ref, s32[16,128]{1,0:T(8,128)} %get-tuple-element.19.num_ref, f32[3,24,128]{2,1,0:T(8,128)} %get-tuple-element.15.mov_ref, f32[8,3,24,128]{3,2,1,0:T(8,128)} %get-tuple-element.20.allm_ref, ...), custom_call_target="tpu_custom_call" | custom-call | tf_op jit(solution)/shard_map/blend/pallas_call | solution.py:574
  79.5 0.0 copy-done.1
  79.5 0.6 copy.14
  (7 shorter events, 0.0 us)
Async XLA Ops:
  0.6 0.8 copy-start
  1.4 0.7 copy-start.2
  1.4 0.7 copy-start.3
  2.2 0.7 copy-start.6
  2.8 0.7 copy-start.5
  3.4 0.7 copy-start.4
  61.0 18.5 %copy-start.1 = (f32[24,128]{1,0:T(8,128)S(1)}, f32[24,128]{1,0:T(8,128)}, u32[]{:S(2)}) copy-start(f32[24,128]{1,0:T(8,128)} %get-tuple-element.16) | copy-start | bytes 36868

commit v3 on v2

--- a/solution.py
+++ b/solution.py
@@ -12,7 +12,8 @@
 SUPPORT = 1.25
 CULL = SUPPORT * SUPPORT * 1.0001
 FAR = 1.0e9
-UNROLL = 16
+UNROLL = 8
+JOIN = 2
 ENTRY_UNROLL = 4
 F32 = jnp.float32
 I32 = jnp.int32
@@ -193,7 +194,7 @@
     sem,
 ):
     radial = base_ref.shape[1]
-    npat = radial
+    npat = radial // JOIN
     lane8 = iota((8, 128), 1)
     sub8 = iota((8, 128), 0)
     blocks_of_lanes = lane8 // 16
@@ -234,8 +235,12 @@
         full = node[c]
         lo = jnp.min(full, axis=1, keepdims=True)
         hi = jnp.max(full, axis=1, keepdims=True)
-        box[2 * c] = jnp.broadcast_to(lo[:, :, None], (npat, 8, 128))
-        box[2 * c + 1] = jnp.broadcast_to(hi[:, :, None], (npat, 8, 128))
+        for q in range(npat):
+            mine = slice(q * JOIN, (q + 1) * JOIN)
+            least = jnp.min(lo[mine], axis=0, keepdims=True)
+            most = jnp.max(hi[mine], axis=0, keepdims=True)
+            box[2 * c, q] = jnp.broadcast_to(least, (8, 128))
+            box[2 * c + 1, q] = jnp.broadcast_to(most, (8, 128))
         lows.append(jnp.min(lo, axis=0, keepdims=True))
         highs.append(jnp.max(hi, axis=0, keepdims=True))
 
@@ -255,6 +260,7 @@
     groups = (jnp.max(total) + 7) // 8
 
     shift[...] = jnp.zeros(shift.shape, F32)
+    cntv[...] = jnp.zeros(cntv.shape, I32)
     wide = npat * 8
     lane_w = iota((wide, 128), 1)
 
@@ -285,7 +291,7 @@
             basec[...] = after
 
         most = jnp.max(basec[...].reshape(npat, 8, 128), axis=1)
-        cntv[...] = most
+        cntv[0:npat, :] = most
         copy = pltpu.make_async_copy(cntv, cnts, sem)
         copy.start()
         copy.wait()
@@ -294,7 +300,13 @@
         def _(p):
             n = jnp.minimum(cnts[p, 0] - 128 * page, 128)
             turns = (jnp.maximum(n, 0) + (UNROLL - 1)) // UNROLL
-            at = [jnp.broadcast_to(node[c, pl.ds(p, 1), :] * 0.8, (8, 128)) for c in range(3)]
+            at = [
+                [
+                    jnp.broadcast_to(node[c, pl.ds(p * JOIN + m, 1), :] * 0.8, (8, 128))
+                    for c in range(3)
+                ]
+                for m in range(JOIN)
+            ]
             first = pl.multiple_of(p * 8, 8)
             cols = [out[c, pl.ds(first, 8), :] for c in range(6)]
             cols = [v * 0.8 for v in cols[:3]] + cols[3:]
@@ -304,20 +316,25 @@
                 for u in range(UNROLL):
                     idx = jnp.full((8, 128), i * UNROLL + u, I32)
                     px, py, pz, wx, wy, wz = [take_lanes(v, idx) for v in cols]
-                    dx = at[0] - px
-                    dy = at[1] - py
-                    dz = at[2] - pz
-                    sq = jnp.maximum(dx * dx + dy * dy + dz * dz, 1e-30)
-                    near = jnp.maximum(1.0 - sq * lax.rsqrt(sq), 0.0)
-                    two = near * near
-                    phi = two * two * (5.0 - 4.0 * near)
-                    acc = [acc[0] + wx * phi, acc[1] + wy * phi, acc[2] + wz * phi]
+                    for m in range(JOIN):
+                        dx = at[m][0] - px
+                        dy = at[m][1] - py
+                        dz = at[m][2] - pz
+                        sq = jnp.maximum(dx * dx + dy * dy + dz * dz, 1e-30)
+                        near = jnp.maximum(1.0 - sq * lax.rsqrt(sq), 0.0)
+                        two = near * near
+                        phi = two * two * (5.0 - 4.0 * near)
+                        acc[3 * m] = acc[3 * m] + wx * phi
+                        acc[3 * m + 1] = acc[3 * m + 1] + wy * phi
+                        acc[3 * m + 2] = acc[3 * m + 2] + wz * phi
                 return tuple(acc)
 
             zero = jnp.zeros((8, 128), F32)
-            acc = lax.fori_loop(0, turns, step, (zero, zero, zero))
-            for c in range(3):
-                shift[c, pl.ds(p, 1), :] += jnp.sum(acc[c], axis=0, keepdims=True)
+            acc = lax.fori_loop(0, turns, step, (zero,) * (3 * JOIN))
+            for m in range(JOIN):
+                for c in range(3):
+                    total_c = jnp.sum(acc[3 * m + c], axis=0, keepdims=True)
+                    shift[c, pl.ds(p * JOIN + m, 1), :] += total_c
 
         return page + 1, jnp.max(most)
 
@@ -538,9 +555,9 @@
             pltpu.VMEM((6, nd * rows, 128), F32),
             pltpu.VMEM((6, 128, 128), F32),
             pltpu.VMEM((3, radial, 128), F32),
-            pltpu.VMEM((6, radial, 8, 128), F32),
-            pltpu.VMEM((6, radial * 8, 128), F32),
-            pltpu.VMEM((radial * 8, 128), I32),
+            pltpu.VMEM((6, radial // JOIN, 8, 128), F32),
+            pltpu.VMEM((6, radial // JOIN * 8, 128), F32),
+            pltpu.VMEM((radial // JOIN * 8, 128), I32),
             pltpu.VMEM((radial, 128), I32),
             pltpu.SMEM((radial, 128), I32),
             pltpu.VMEM((3, radial, 128), F32),

time: 81.3 us -> 77.6 us (0.954)
  Pallas kernels: 74.8 us -> 71.7 us
    pallas_call x1, Pallas kernels: 24.5 us -> 18.9 us  [local(): pl.pallas_call(functools.partial(rbf_kernel, nd, rows, ng, lrows), out_sh...]
    pallas_call x1, Pallas kernels: 11 us -> 13.3 us  [local(): pl.pallas_call(functools.partial(metric_kernel, nb, ng), out_shape=(sds((...]
where the time goes in v3:
time: 77.6 us; the launch traced here: 77.1 us
  Pallas kernels  71.7 us (92%)
  local copies, waits for them, and re-layouts  3.16 us (4%)
  other arithmetic  1.33 us (2%)
  between operations  0.88 us (1%)
    pallas_call x1, Pallas kernels, local(): pl.pallas_call(functools.partial(gather_kernel, nb, ng), out_shape=(sds((...  20.8 us
    pallas_call x1, Pallas kernels, local(): pl.pallas_call(functools.partial(rbf_kernel, nd, rows, ng, lrows), out_sh...  18.9 us
    pallas_call x1, Pallas kernels, local(): pl.pallas_call(blend_kernel, out_shape=sds((nvar, radial, lines), F32), i...  18.8 us
    pallas_call x1, Pallas kernels, local(): pl.pallas_call(functools.partial(metric_kernel, nb, ng), out_shape=(sds((...  13.3 us
    unnamed x15, local copies, waits for them, and re-layouts  2.55 us

profile of v3, /device:TPU:0, one launch (start us, length us, event | category | flops | bytes accessed | tf_op | source)
XLA Modules:
  0.0 77.1 jit_solution(4985743306762702514)
XLA Ops:
  0.6 0.0 copy-start
  0.9 0.1 broadcast_add_fusion
  0.9 0.5 copy-done
  1.4 0.0 copy-start.2
  1.4 0.0 copy-start.3
  1.4 0.6 fusion.base_ref
  2.0 0.1 copy-done.2
  2.1 0.0 copy-done.3
  2.2 0.0 copy-start.6
  2.2 0.6 reshape.219.pts_ref
  2.8 0.0 copy-start.5
  2.8 0.1 copy-done.6
  2.8 0.6 copy-done.5
  3.4 0.0 copy-start.4
  3.4 0.7 copy-done.4
  4.1 0.6 pad_add_fusion.lst_ref
  4.7 20.8 %gather_points.1 = (f32[32,24,128]{2,1,0:T(8,128)}, s32[8,6,128]{2,1,0:T(8,128)}, f32[8,5,24,128]{3,2,1,0:T(8,128)}) custom-call(f32[24,128]{1,0:T(8,128)} %reshape.219.pts_ref, s32[6,128]{1,0:T(8,128)} %pad_add_fusion.lst_ref, f32[5,24,128]{2,1,0:T(8,128)} %bitcast.25), custom_call_target="tpu_custom_call" | custom-call | tf_op jit(solution)/shard_map/gather_points/pallas_call | solution.py:530
  25.5 18.9 %move_nodes.1 = (f32[3,24,128]{2,1,0:T(8,128)}, s32[16,128]{1,0:T(8,128)}, s32[16,128]{1,0:T(8,128)}, s32[16,128]{1,0:T(8,128)}) custom-call(s32[1]{0:T(128)} %bitcast.here_ref, f32[3,24,128]{2,1,0:T(8,128)} %fusion.base_ref, f32[32,24,128]{2,1,0:T(8,128)} %get-tuple-element.13.pts_ref, s32[8,6,128]{2,1,0:T(8,128)} %get-tuple-element.14.lst_ref), custom_call_target="tpu_custom_call" | custom-call | flops 200000000 | bytes 500000 | tf_op jit(solution)/shard_map/move_nodes/pallas_call | solution.py:544
  44.5 13.3 %metric.1 = (f32[24,128]{1,0:T(8,128)}, f32[8,3,24,128]{3,2,1,0:T(8,128)}, f32[8,24,128]{2,1,0:T(8,128)}) custom-call(f32[3,24,128]{2,1,0:T(8,128)} %get-tuple-element.15.mov_ref), custom_call_target="tpu_custom_call" | custom-call | tf_op jit(solution)/shard_map/metric/pallas_call | solution.py:570
  57.7 0.0 copy-start.1
  57.7 18.8 %blend.1 = f32[5,24,128]{2,1,0:T(8,128)} custom-call(s32[16,128]{1,0:T(8,128)} %get-tuple-element.17.don_ref, s32[16,128]{1,0:T(8,128)} %get-tuple-element.18.rec_ref, s32[16,128]{1,0:T(8,128)} %get-tuple-element.19.num_ref, f32[3,24,128]{2,1,0:T(8,128)} %get-tuple-element.15.mov_ref, f32[8,3,24,128]{3,2,1,0:T(8,128)} %get-tuple-element.20.allm_ref, ...), custom_call_target="tpu_custom_call" | custom-call | tf_op jit(solution)/shard_map/blend/pallas_call | solution.py:591
  76.5 0.0 copy-done.1
  76.5 0.6 copy.14
  (7 shorter events, 0.0 us)
Async XLA Ops:
  0.6 0.8 %copy-start = (f32[1,3,1,24,128]{4,3,2,1,0:T(8,128)S(1)}, f32[1,3,1,24,128]{4,3,2,1,0:T(8,128)}, u32[]{:S(2)}) copy-start(f32[1,3,1,24,128]{4,3,2,1,0:T(8,128)} %param.7) | copy-start | bytes 110596
  1.4 0.7 copy-start.2
  1.4 0.7 copy-start.3
  2.2 0.7 copy-start.6
  2.8 0.7 copy-start.5
  3.4 0.7 copy-start.4
  57.7 18.8 %copy-start.1 = (f32[24,128]{1,0:T(8,128)S(1)}, f32[24,128]{1,0:T(8,128)}, u32[]{:S(2)}) copy-start(f32[24,128]{1,0:T(8,128)} %get-tuple-element.16) | copy-start | bytes 36868
